TPU v7x, 32 devices: a whole 2x2x4 slice. The times are simulated.
32 devices in a mesh: groups: 2 (over y), seq: 8 (over z, x), head: 2 (over core).
Axes of the slice: x: 2, y: 2, z: 4, core: 2. Of those that a mesh axis runs over, the one named last changes fastest.
Arguments:
- queries: bfloat16 [2048, 1024], P(('groups', 'seq'), 'head'), parts along dimension 0, may hold values from -600 to 600
- keys: bfloat16 [2048, 1024], P(('groups', 'seq'), 'head'), parts along dimension 0, may hold values from -600 to 600
- values: bfloat16 [2048, 1024], P(('groups', 'seq'), 'head'), parts along dimension 0, may hold values from -600 to 600
- out_weight: bfloat16 [2048, 1024], P('seq', 'head'), may hold values from -0.1875 to 0.1875
- grad_y: bfloat16 [2048, 2048], P(('groups', 'seq')), parts along dimension 0, may hold values from -6 to 6
Outputs:
- out_y: bfloat16 [2048, 2048], P(('groups', 'seq')), parts along dimension 0
- grad_queries: bfloat16 [2048, 1024], P(('groups', 'seq'), 'head'), parts along dimension 0
- grad_keys: bfloat16 [2048, 1024], P(('groups', 'seq'), 'head'), parts along dimension 0
- grad_values: bfloat16 [2048, 1024], P(('groups', 'seq'), 'head'), parts along dimension 0
- grad_weight: float32 [4096, 1024], P(('groups', 'seq'), 'head'), parts along dimension 0
There are 2 independent parts, one for each index of `groups`. A program takes and returns all parts, laid end to end along the dimension named above; an argument that names none is the same for every part. Nothing has to cross between parts.
All inputs are finite; a program needn't handle non-finite values.
Results may differ from a plain program's by a relative error of at most 0.009.
Values may be sent and summed in bfloat16 or wider, within the bound.
No kernel may reach another device: no remote copies, remote signals or barrier semaphores. Data moves between devices by JAX's collectives and lax.ppermute only.
A program may use at most 192 MiB of HBM per device.

v0:
```python
import jax
import jax.numpy as jnp
from jax import lax
from jax.sharding import PartitionSpec as P

DH = 128
TILE = 128
epsilon = 1e-06


def carried_in(value, axis, join, neutral, backward):
    count, mine = (lax.axis_size(axis), lax.axis_index(axis))
    pieces = lax.all_gather(value, axis)
    if backward:
        pieces = pieces[::-1]
        mine = count - 1 - mine
    so_far = jnp.full_like(value, 0) + jnp.asarray(neutral, value.dtype)

    def turn(position, so_far):
        longer = join(so_far, pieces[position])
        return jnp.where(position < mine, longer, so_far)

    return lax.fori_loop(0, count - 1, turn, so_far)


def add_states(earlier, later):
    return earlier + later


def on_device(queries, keys, values, out_weight, grad_y):
    row_count = queries.shape[0]
    tile_count = row_count // TILE
    head_count = queries.shape[1] // DH

    def tiled(array):
        return array.reshape(tile_count, TILE, head_count, DH)

    query_tiles = tiled(queries)
    key_tiles = tiled(keys)
    value_tiles = tiled(values)
    causal = lax.broadcasted_iota(jnp.int32, (TILE, TILE), 0) >= lax.broadcasted_iota(
        jnp.int32, (TILE, TILE), 1
    )
    raw_scores = jnp.einsum(
        "nthd,nshd->nhts", query_tiles, key_tiles, preferred_element_type=jnp.float32
    )
    scores = jnp.where(causal, raw_scores, 0.0).astype(jnp.bfloat16)
    states = jnp.einsum(
        "nshd,nshe->nhde", key_tiles, value_tiles, preferred_element_type=jnp.float32
    )
    empty_state = jnp.zeros(states.shape[1:], jnp.float32)
    device_prefix = carried_in(jnp.sum(states, axis=0), "seq", add_states, empty_state, False)
    prefix_state = (device_prefix[None] + (jnp.cumsum(states, axis=0) - states)).astype(
        jnp.bfloat16
    )
    attended = jnp.einsum(
        "nhts,nshe->nthe", scores, value_tiles, preferred_element_type=jnp.float32
    )
    attended = attended + jnp.einsum(
        "nthd,nhde->nthe", query_tiles, prefix_state, preferred_element_type=jnp.float32
    )
    inverse_rms = lax.rsqrt(jnp.mean(attended * attended, axis=-1, keepdims=True) + epsilon)
    normed_exact = attended * inverse_rms
    normed = normed_exact.astype(jnp.bfloat16).reshape(row_count, -1)
    contract_last = (((1,), (1,)), ((), ()))
    back_weight = lax.all_gather(out_weight, "seq", axis=0, tiled=True)
    grad_normed = jnp.dot(grad_y, back_weight, preferred_element_type=jnp.float32)
    fore_weight = lax.all_gather(out_weight, "seq", axis=0, tiled=True)
    partial_out = lax.dot_general(
        normed, fore_weight, contract_last, preferred_element_type=jnp.float32
    )
    out_y = lax.psum(partial_out.astype(jnp.bfloat16), "head")
    grad_tiles = tiled(grad_normed)
    projected = jnp.mean(grad_tiles * normed_exact, axis=-1, keepdims=True)
    grad_out = (inverse_rms * (grad_tiles - normed_exact * projected)).astype(jnp.bfloat16)
    raw_grad = jnp.einsum(
        "nthe,nshe->nhts", grad_out, value_tiles, preferred_element_type=jnp.float32
    )
    grad_scores = jnp.where(causal, raw_grad, 0.0).astype(jnp.bfloat16)
    adjoint = jnp.einsum(
        "nthd,nthe->nhde", query_tiles, grad_out, preferred_element_type=jnp.float32
    )
    own_adjoint = jnp.sum(adjoint, axis=0)
    device_suffix = carried_in(own_adjoint, "seq", add_states, empty_state, True)
    later_tiles = jnp.flip(jnp.cumsum(jnp.flip(adjoint, 0), axis=0), 0) - adjoint
    suffix_state = (device_suffix[None] + later_tiles).astype(jnp.bfloat16)
    grad_queries = jnp.einsum(
        "nhts,nshd->nthd", grad_scores, key_tiles, preferred_element_type=jnp.float32
    )
    grad_queries = grad_queries + jnp.einsum(
        "nthe,nhde->nthd", grad_out, prefix_state, preferred_element_type=jnp.float32
    )
    grad_keys = jnp.einsum(
        "nhts,nthd->nshd", grad_scores, query_tiles, preferred_element_type=jnp.float32
    )
    grad_keys = grad_keys + jnp.einsum(
        "nshe,nhde->nshd", value_tiles, suffix_state, preferred_element_type=jnp.float32
    )
    grad_values = jnp.einsum(
        "nhts,nthe->nshe", scores, grad_out, preferred_element_type=jnp.float32
    )
    grad_values = grad_values + jnp.einsum(
        "nshd,nhde->nshe", key_tiles, suffix_state, preferred_element_type=jnp.float32
    )
    grad_weight = lax.psum_scatter(
        lax.dot_general(
            grad_y, normed, (((0,), (0,)), ((), ())), preferred_element_type=jnp.float32
        ),
        "seq",
        scatter_dimension=0,
        tiled=True,
    )
    return (
        out_y,
        grad_queries.reshape(row_count, -1).astype(jnp.bfloat16),
        grad_keys.reshape(row_count, -1).astype(jnp.bfloat16),
        grad_values.reshape(row_count, -1).astype(jnp.bfloat16),
        grad_weight,
    )


def solution(mesh):
    placed = (
        P(("groups", "seq"), "head"),
        P(("groups", "seq"), "head"),
        P(("groups", "seq"), "head"),
        P("seq", "head"),
        P(("groups", "seq"), None),
    )
    return jax.shard_map(
        on_device,
        mesh=mesh,
        in_specs=placed,
        out_specs=(
            P(("groups", "seq"), None),
            P(("groups", "seq"), "head"),
            P(("groups", "seq"), "head"),
            P(("groups", "seq"), "head"),
            P(("groups", "seq"), "head"),
        ),
        check_vma=False,
    )
```

profile of v0, /device:TPU:0, one launch (start us, length us, event | category | flops | bytes accessed | tf_op | source)
XLA Modules:
  0.0 284.6 jit_solution(14528810327368836696)
XLA Ops:
  7.2 0.0 copy-start
  7.2 0.0 all-gather.8.cloned.1.call-start
  7.2 1.1 copy.104
  8.3 0.0 copy-start.4
  8.3 1.8 fusion.10
  10.1 0.0 all-gather.8.cloned.1.call-update
  10.2 0.0 all-gather.6.cloned.1.call-start
  10.2 0.7 all-gather.6.cloned.1.call-update
  10.9 0.0 all-gather.10.cloned.1.call-start
  11.0 1.2 fusion.1
  12.2 0.6 copy-done.9
  12.8 1.1 convolution_bitcast_fusion.4
  14.0 0.0 copy-start.2
  14.0 48.7 %all-gather.8.cloned.1.call-done = f32[32,128,128]{2,1,0:T(8,128)} async-done(((f32[4,128,128]{2,1,0:T(8,128)}), f32[32,128,128]{2,1,0:T(8,128)}) %all-gather.8.cloned.1.call-update) | async-done | bytes 2097168 | tf_op jit(solution)/shard_map/all_gather | solution.py:13
  62.7 7.5 %while.28 = (s32[]{:T(128)}, f32[4,128,128]{2,1,0:T(8,128)S(1)}, s32[]{:T(128)}, f32[8,4,128,128]{3,2,1,0:T(8,128)}, s32[]{:T(128)}, /*index=5*/s32[]{:T(128)}) while((s32[]{:T(128)}, f32[4,128,128]{2,1,0:T(8,128)S(1)}, s32[]{:T(128)}, f32[8,4,128,128]{3,2,1,0:T(8,128)}, s32[]{:T(128)}, /*index=5*/s32[]{:T(128)}) %tuple.84), condition=%wide.region_1.2_spmd.clone, body=%wide.region_0.1_spmd.clone.sunk | while | flops 196612 | bytes 786533 | solution.py:23
  62.7 1.1 add_select_fusion.4
  63.8 1.0 add_select_fusion.4
  64.9 1.0 add_select_fusion.4
  66.0 1.0 add_select_fusion.4
  67.0 1.0 add_select_fusion.4
  68.1 1.0 add_select_fusion.4
  69.2 1.0 add_select_fusion.4
  70.3 0.3 multiply_reduce_fusion.1
  70.5 42.1 %all-gather.6.cloned.1.call-done = bf16[2048,512]{1,0:T(8,128)(2,1)} async-done(((bf16[256,512]{1,0:T(8,128)(2,1)}), bf16[2048,512]{1,0:T(8,128)(2,1)}) %all-gather.6.cloned.1.call-update) | async-done | bytes 2097168 | tf_op jit(solution)/shard_map/all_gather | solution.py:68
  112.7 2.5 fusion.28
  115.2 0.1 fusion.6
  115.3 0.0 copy-start.6
  115.3 0.2 convolution_bitcast_fusion.2
  115.5 0.8 copy.47
  116.3 0.0 all-gather.10.cloned.1.call-update
  116.4 0.0 reduce-scatter.2.cloned.1.call-start
  116.4 2.7 convolution_bitcast_fusion
  119.1 0.0 reduce-scatter.2.cloned.1.call-update
  119.1 0.0 all-reduce.2.cloned.1.call-start
  119.2 0.8 copy-done.3
  120.0 0.2 fusion.2
  120.2 0.0 copy-start.10
  120.2 1.2 convolution_bitcast_fusion.3
  121.4 0.8 fusion.3
  122.2 1.7 copy.52
  123.9 1.9 convolution_bitcast_fusion.1
  125.8 1.8 fusion.29
  127.6 2.5 convolution_convert_fusion
  130.1 0.0 all-reduce.2.cloned.1.call-update
  130.2 34.2 %all-gather.10.cloned.1.call-done = f32[32,128,128]{2,1,0:T(8,128)} async-done(((f32[4,128,128]{2,1,0:T(8,128)}), f32[32,128,128]{2,1,0:T(8,128)}) %all-gather.10.cloned.1.call-update) | async-done | bytes 2097168 | tf_op jit(solution)/shard_map/all_gather | solution.py:13
  164.3 1.7 rev.3
  166.1 0.8 while.29
  166.1 0.1 add_select_fusion.5
  166.2 0.1 add_select_fusion.5
  166.3 0.1 add_select_fusion.5
  166.4 0.1 add_select_fusion.5
  166.5 0.1 add_select_fusion.5
  166.7 0.1 add_select_fusion.5
  166.8 0.1 add_select_fusion.5
  166.9 0.0 copy-start.8
  166.9 0.1 copy.48
  167.1 1.2 fusion.4
  168.2 0.8 copy.53
  169.0 0.2 fusion.5
  169.2 0.8 copy.54
  170.0 84.8 %reduce-scatter.2.cloned.1.call-done = f32[256,512]{0,1:T(8,128)} async-done(((f32[2048,512]{0,1:T(8,128)}), f32[256,512]{0,1:T(8,128)}) %reduce-scatter.2.cloned.1.call-update) | async-done | bytes 524304 | tf_op jit(solution)/shard_map/reduce_scatter | solution.py:105
  254.8 2.0 copy.55
  256.8 19.4 %all-reduce.2.cloned.1.call-done = bf16[128,2048]{1,0:T(8,128)(2,1)} async-done(((bf16[128,2048]{1,0:T(8,128)(2,1)}), bf16[128,2048]{1,0:T(8,128)(2,1)}) %all-reduce.2.cloned.1.call-update) | async-done | bytes 524304 | tf_op jit(solution)/shard_map/psum | solution.py:72
  276.2 1.9 copy.120
  (22 shorter events, 0.2 us)
Async XLA Ops:
  7.2 105.5 %copy-start = (bf16[128,2048]{1,0:T(8,128)(2,1)S(1)}, bf16[128,2048]{1,0:T(8,128)(2,1)}, u32[]{:S(2)}) copy-start(bf16[128,2048]{1,0:T(8,128)(2,1)} %param.13) | copy-start | bytes 1572868
  7.2 55.6 %all-gather.8.cloned.1.call-start = ((), (), s32[]{:S(2)}) async-start(), calls=%async_computation.4 | async-start | bytes 2359296 | tf_op jit(solution)/shard_map/all_gather | solution.py:13
  8.3 2.6 copy-start.4
  10.2 102.5 %all-gather.6.cloned.1.call-start = ((), (), s32[]{:S(2)}) async-start(), calls=%async_computation.1 | async-start | bytes 2359296 | tf_op jit(solution)/shard_map/all_gather | solution.py:68
  10.9 153.4 %all-gather.10.cloned.1.call-start = ((), (), s32[]{:S(2)}) async-start(), calls=%async_computation.5 | async-start | bytes 2359296 | tf_op jit(solution)/shard_map/all_gather | solution.py:13
  12.2 0.6 copy-start.9
  14.0 56.2 %copy-start.2 = (f32[4,128,128]{2,1,0:T(8,128)S(1)}, f32[4,128,128]{2,1,0:T(8,128)}, u32[]{:S(2)}) copy-start(f32[4,128,128]{2,1,0:T(8,128)} %fusion.10) | copy-start | bytes 786436
  62.7 7.5 %copy-start.5 = (bf16[128,512]{1,0:T(8,128)(2,1)S(1)}, bf16[128,512]{1,0:T(8,128)(2,1)}, u32[]{:S(2)}) copy-start(bf16[128,512]{1,0:T(8,128)(2,1)} %param.9) | copy-start | bytes 393220
  115.3 3.7 %copy-start.6 = (bf16[1,128,4,128]{1,3,2,0:T(8,128)(2,1)}, bf16[1,128,4,128]{1,3,2,0:T(8,128)(2,1)S(1)}, u32[]{:S(2)}) copy-start(bf16[1,128,4,128]{1,3,2,0:T(8,128)(2,1)S(1)} %get-tuple-element.222) | copy-start | bytes 393220
  116.4 138.5 %reduce-scatter.2.cloned.1.call-start = ((), (), s32[]{:S(2)}) async-start(), calls=%async_computation.3 | async-start | bytes 4718592 | tf_op jit(solution)/shard_map/reduce_scatter | solution.py:105
  119.1 0.9 copy-start.3
  119.1 8.5 %copy-start.1 = (bf16[2048,512]{1,0:T(8,128)(2,1)S(1)}, bf16[2048,512]{1,0:T(8,128)(2,1)}, u32[]{:S(2)}) copy-start(bf16[2048,512]{1,0:T(8,128)(2,1)} %all-gather.6.cloned.1.call-done) | copy-start | bytes 6291460
  119.1 157.1 %all-reduce.2.cloned.1.call-start = ((), (), s32[]{:S(2)}) async-start(), calls=%async_computation.2 | async-start | bytes 1048576 | tf_op jit(solution)/shard_map/psum | solution.py:72
  120.2 2.0 copy-start.10
  166.1 2.9 %copy-start.7 = (f32[4,128,128]{2,1,0:T(8,128)S(1)}, f32[4,128,128]{2,1,0:T(8,128)}, u32[]{:S(2)}) copy-start(f32[4,128,128]{2,1,0:T(8,128)} %fusion.29) | copy-start | bytes 786436
  166.9 2.2 copy-start.8
Sparse Core Ops, SparseCore 0:
  10.7 51.9 all-gather.7
  64.9 47.7 all-gather.5
  116.5 47.8 all-gather.9
  167.8 86.9 reduce-scatter.1
  257.7 18.4 all-reduce.1
where the time goes:
time: 285 us
  waiting for transfers between devices  230 us (81%)
  matrix products  19.6 us (7%)
  between operations  14 us (5%)
  local copies, waits for them, and re-layouts  12.4 us (4%)
  other arithmetic  8.1 us (3%)
    reduce_scatter x1, waiting for transfers between devices, on_device(): lax.psum_scatter(lax.dot_general(grad_y, normed, (((0,), (0,)), ((), ()))...  84.8 us
    all_gather x2, waiting for transfers between devices, carried_in(): pieces = lax.all_gather(value, axis)  82.9 us
    all_gather x1, waiting for transfers between devices, on_device(): fore_weight = lax.all_gather(out_weight, 'seq', axis=0, tiled=True)  42.1 us
    psum x1, waiting for transfers between devices, on_device(): out_y = lax.psum(partial_out.astype(jnp.bfloat16), 'head')  19.4 us
    unnamed x27, local copies, waits for them, and re-layouts  8.63 us
    select_n x14, other arithmetic, turn(): return jnp.where(position < mine, longer, so_far)  7.89 us
  transfers between devices with their start and end apart: 5, of which 5 were waited for; matrix products, arithmetic and copies ran while one was open for 11% of the time, Pallas kernels for 0%

commit v1 on v0

--- a/solution.py
+++ b/solution.py
@@ -65,7 +65,13 @@
     contract_last = (((1,), (1,)), ((), ()))
     back_weight = lax.all_gather(out_weight, "seq", axis=0, tiled=True)
     grad_normed = jnp.dot(grad_y, back_weight, preferred_element_type=jnp.float32)
-    fore_weight = lax.all_gather(out_weight, "seq", axis=0, tiled=True)
+    size = lax.axis_size("seq")
+    block, parts = (out_weight, [out_weight])
+    for _ in range(size - 1):
+        block = lax.ppermute(block, "seq", [(i, (i + 1) % size) for i in range(size)])
+        parts.insert(0, block)
+    row_of_blocks = jnp.concatenate(parts, axis=0)
+    fore_weight = jnp.roll(row_of_blocks, (lax.axis_index("seq") + 1) * out_weight.shape[0], axis=0)
     partial_out = lax.dot_general(
         normed, fore_weight, contract_last, preferred_element_type=jnp.float32
     )

time: 285 us -> 304 us (1.067)
  waiting for transfers between devices: 230 us -> 245 us
  local copies, waits for them, and re-layouts: 12.4 us -> 16.2 us
    ppermute x0 -> x7, waiting for transfers between devices: none -> 85.8 us  [on_device(): lax.ppermute(block, 'seq', [(i, (i + 1) % size) for i in range(size)])]
    reduce_scatter x1, waiting for transfers between devices: 84.8 us -> 47.8 us  [on_device(): lax.psum_scatter(lax.dot_general(grad_y, normed, (((0,), (0,)), ((), ()))...]
    all_gather x2, waiting for transfers between devices: 82.9 us -> 49.5 us  [carried_in(): pieces = lax.all_gather(value, axis)]
    unnamed x27 -> x34, local copies, waits for them, and re-layouts: 8.63 us -> 12.4 us
  transfers between devices with their start and end apart: 5 -> 12, of which waited for: 5 -> 11; matrix products, arithmetic and copies ran while one was open for 11% -> 10% of each run, Pallas kernels for 0% -> 0%
where the time goes in v1:
time: 304 us; the launch traced here: 303 us
  waiting for transfers between devices  245 us (81%)
  matrix products  17.7 us (6%)
  local copies, waits for them, and re-layouts  16.2 us (5%)
  between operations  14.1 us (5%)
  other arithmetic  8.07 us (3%)
    ppermute x7, waiting for transfers between devices, on_device(): lax.ppermute(block, 'seq', [(i, (i + 1) % size) for i in range(size)])  85.8 us
    all_gather x2, waiting for transfers between devices, carried_in(): pieces = lax.all_gather(value, axis)  49.5 us
    reduce_scatter x1, waiting for transfers between devices, on_device(): lax.psum_scatter(lax.dot_general(grad_y, normed, (((0,), (0,)), ((), ()))...  47.8 us
    all_gather x1, waiting for transfers between devices, on_device(): back_weight = lax.all_gather(out_weight, 'seq', axis=0, tiled=True)  42.2 us
    psum x1, waiting for transfers between devices, on_device(): out_y = lax.psum(partial_out.astype(jnp.bfloat16), 'head')  19.4 us
    unnamed x34, local copies, waits for them, and re-layouts  12.4 us
    select_n x14, other arithmetic, turn(): return jnp.where(position < mine, longer, so_far)  7.85 us
  transfers between devices with their start and end apart: 12, of which 11 were waited for; matrix products, arithmetic and copies ran while one was open for 10% of the time, Pallas kernels for 0%

profile of v1, /device:TPU:0, one launch (start us, length us, event | category | flops | bytes accessed | tf_op | source)
XLA Modules:
  0.0 303.4 jit_solution(9923882286460450453)
XLA Ops:
  7.2 1.1 copy.104
  8.3 1.8 fusion.11
  10.1 0.0 all-gather.6.cloned.1.call-start
  10.2 0.7 all-gather.6.cloned.1.call-update
  11.0 1.2 fusion.2
  12.2 1.1 convolution_bitcast_fusion.4
  13.3 49.4 %all-gather.8.cloned.1.call-done = f32[32,128,128]{2,1,0:T(8,128)} async-done(((f32[4,128,128]{2,1,0:T(8,128)}), f32[32,128,128]{2,1,0:T(8,128)}) %all-gather.8.cloned.1.call-update) | async-done | bytes 2097168 | tf_op jit(solution)/shard_map/all_gather | solution.py:13
  62.7 7.4 %while.28 = (s32[]{:T(128)}, f32[4,128,128]{2,1,0:T(8,128)S(1)}, s32[]{:T(128)}, f32[8,4,128,128]{3,2,1,0:T(8,128)}, s32[]{:T(128)}, /*index=5*/s32[]{:T(128)}) while((s32[]{:T(128)}, f32[4,128,128]{2,1,0:T(8,128)S(1)}, s32[]{:T(128)}, f32[8,4,128,128]{3,2,1,0:T(8,128)}, s32[]{:T(128)}, /*index=5*/s32[]{:T(128)}) %tuple.84), condition=%wide.region_1.2_spmd.clone, body=%wide.region_0.1_spmd.clone.sunk | while | flops 196612 | bytes 786525 | solution.py:23
  62.7 1.0 add_select_fusion.4
  63.8 1.0 add_select_fusion.4
  64.9 1.0 add_select_fusion.4
  65.9 1.0 add_select_fusion.4
  67.0 1.0 add_select_fusion.4
  68.1 1.0 add_select_fusion.4
  69.1 1.0 add_select_fusion.4
  70.2 0.3 multiply_reduce_fusion.1
  70.5 42.2 %all-gather.6.cloned.1.call-done = bf16[2048,512]{1,0:T(8,128)(2,1)} async-done(((bf16[256,512]{1,0:T(8,128)(2,1)}), bf16[2048,512]{1,0:T(8,128)(2,1)}) %all-gather.6.cloned.1.call-update) | async-done | bytes 2097168 | tf_op jit(solution)/shard_map/all_gather | solution.py:66
  112.7 2.5 fusion.30
  115.2 0.1 multiply_reduce_fusion
  115.3 0.1 fusion.7
  115.3 0.2 convolution_bitcast_fusion.2
  115.5 0.8 copy.47
  116.4 0.0 reduce-scatter.2.cloned.1.call-start
  116.4 2.6 convolution_bitcast_fusion
  119.1 0.0 all-reduce.2.cloned.1.call-start
  119.2 0.6 collective-permute-start
  119.8 9.6 %collective-permute-done = bf16[256,512]{1,0:T(8,128)(2,1)S(1)} collective-permute-done((bf16[256,512]{1,0:T(8,128)(2,1)S(1)}, bf16[256,512]{1,0:T(8,128)(2,1)S(1)}, u32[]{:S(2)}, u32[]{:S(2)}) %collective-permute-start) | collective-permute-done | bytes 262176 | tf_op jit(solution)/shard_map/ppermute | solution.py:71
  129.3 0.8 collective-permute-start.1
  130.1 12.8 %collective-permute-done.1 = bf16[256,512]{1,0:T(8,128)(2,1)S(1)} collective-permute-done((bf16[256,512]{1,0:T(8,128)(2,1)S(1)}, bf16[256,512]{1,0:T(8,128)(2,1)S(1)}, u32[]{:S(2)}, u32[]{:S(2)}) %collective-permute-start.1) | collective-permute-done | bytes 262176 | tf_op jit(solution)/shard_map/ppermute | solution.py:71
  142.9 13.8 %collective-permute-done.2 = bf16[256,512]{1,0:T(8,128)(2,1)S(1)} collective-permute-done((bf16[256,512]{1,0:T(8,128)(2,1)S(1)}, bf16[256,512]{1,0:T(8,128)(2,1)S(1)}, u32[]{:S(2)}, u32[]{:S(2)}) %collective-permute-start.2) | collective-permute-done | bytes 262176 | tf_op jit(solution)/shard_map/ppermute | solution.py:71
  156.7 13.6 %collective-permute-done.3 = bf16[256,512]{1,0:T(8,128)(2,1)S(1)} collective-permute-done((bf16[256,512]{1,0:T(8,128)(2,1)S(1)}, bf16[256,512]{1,0:T(8,128)(2,1)S(1)}, u32[]{:S(2)}, u32[]{:S(2)}) %collective-permute-start.3) | collective-permute-done | bytes 262176 | tf_op jit(solution)/shard_map/ppermute | solution.py:71
  170.3 10.5 %collective-permute-done.4 = bf16[256,512]{1,0:T(8,128)(2,1)S(1)} collective-permute-done((bf16[256,512]{1,0:T(8,128)(2,1)S(1)}, bf16[256,512]{1,0:T(8,128)(2,1)S(1)}, u32[]{:S(2)}, u32[]{:S(2)}) %collective-permute-start.4) | collective-permute-done | bytes 262176 | tf_op jit(solution)/shard_map/ppermute | solution.py:71
  180.8 9.3 %collective-permute-done.5 = bf16[256,512]{1,0:T(8,128)(2,1)} collective-permute-done((bf16[256,512]{1,0:T(8,128)(2,1)S(1)}, bf16[256,512]{1,0:T(8,128)(2,1)}, u32[]{:S(2)}, u32[]{:S(2)}) %collective-permute-start.5) | collective-permute-done | bytes 262176 | tf_op jit(solution)/shard_map/ppermute | solution.py:71
  190.1 16.2 %collective-permute-done.6 = bf16[256,512]{1,0:T(8,128)(2,1)} collective-permute-done((bf16[256,512]{1,0:T(8,128)(2,1)}, bf16[256,512]{1,0:T(8,128)(2,1)}, u32[]{:S(2)}, u32[]{:S(2)}) %collective-permute-start.6) | collective-permute-done | bytes 262176 | tf_op jit(solution)/shard_map/ppermute | solution.py:71
  206.4 1.0 constant_dynamic-update-slice_fusion.15
  207.3 1.0 constant_dynamic-update-slice_fusion.14
  208.5 1.0 constant_dynamic-update-slice_fusion.7
  209.5 1.0 constant_dynamic-update-slice_fusion.6
  210.6 2.0 copy-done.3
  212.6 0.2 fusion.3
  212.8 0.2 convolution_bitcast_fusion.3
  213.0 0.2 fusion.4
  213.2 0.8 copy.52
  214.0 0.9 convolution_bitcast_fusion.1
  214.9 0.9 fusion.31
  215.8 3.2 %convolution_convert_fusion = bf16[128,2048]{1,0:T(8,128)(2,1)} fusion(bf16[128,512]{0,1:T(8,128)(2,1)S(1)} %bitcast.125, bf16[4096,512]{1,0:T(8,128)(2,1)} %copy-done.3, s32[]{:T(128)S(6)} %select_n.64), kind=kOutput, calls=%fused_computation.3 | convolution fusion | flops 268697600 | bytes 2752516 | tf_op jit(solution)/shard_map/dot_general | solution.py:75
  219.1 1.8 rev.3
  220.9 0.8 while.29
  220.9 0.1 add_select_fusion.5
  221.0 0.1 add_select_fusion.5
  221.1 0.1 add_select_fusion.5
  221.3 0.1 add_select_fusion.5
  221.4 0.1 add_select_fusion.5
  221.5 0.1 add_select_fusion.5
  221.6 0.1 add_select_fusion.5
  221.7 0.1 copy.48
  221.9 1.2 fusion.5
  223.1 0.8 copy.53
  223.8 1.2 fusion.6
  225.0 0.8 copy.54
  225.8 47.8 %reduce-scatter.2.cloned.1.call-done = f32[256,512]{0,1:T(8,128)} async-done(((f32[2048,512]{0,1:T(8,128)}), f32[256,512]{0,1:T(8,128)}) %reduce-scatter.2.cloned.1.call-update) | async-done | bytes 524304 | tf_op jit(solution)/shard_map/reduce_scatter | solution.py:111
  273.6 2.0 copy.55
  275.6 19.4 %all-reduce.2.cloned.1.call-done = bf16[128,2048]{1,0:T(8,128)(2,1)} async-done(((bf16[128,2048]{1,0:T(8,128)(2,1)}), bf16[128,2048]{1,0:T(8,128)(2,1)}) %all-reduce.2.cloned.1.call-update) | async-done | bytes 524304 | tf_op jit(solution)/shard_map/psum | solution.py:78
  295.0 1.9 copy.135
  (44 shorter events, 0.5 us)
Async XLA Ops:
  7.2 105.5 %copy-start = (bf16[128,2048]{1,0:T(8,128)(2,1)S(1)}, bf16[128,2048]{1,0:T(8,128)(2,1)}, u32[]{:S(2)}) copy-start(bf16[128,2048]{1,0:T(8,128)(2,1)} %param.13) | copy-start | bytes 1572868
  7.2 63.1 %copy-start.5 = (bf16[128,512]{1,0:T(8,128)(2,1)S(1)}, bf16[128,512]{1,0:T(8,128)(2,1)}, u32[]{:S(2)}) copy-start(bf16[128,512]{1,0:T(8,128)(2,1)} %param.9) | copy-start | bytes 393220
  7.2 55.6 %all-gather.8.cloned.1.call-start = ((), (), s32[]{:S(2)}) async-start(), calls=%async_computation.4 | async-start | bytes 2359296 | tf_op jit(solution)/shard_map/all_gather | solution.py:13
  10.1 60.1 %copy-start.2 = (f32[4,128,128]{2,1,0:T(8,128)S(1)}, f32[4,128,128]{2,1,0:T(8,128)}, u32[]{:S(2)}) copy-start(f32[4,128,128]{2,1,0:T(8,128)} %fusion.11) | copy-start | bytes 786436
  10.1 102.5 %all-gather.6.cloned.1.call-start = ((), (), s32[]{:S(2)}) async-start(), calls=%async_computation.2 | async-start | bytes 2359296 | tf_op jit(solution)/shard_map/all_gather | solution.py:66
  10.9 208.2 %all-gather.10.cloned.1.call-start = ((), (), s32[]{:S(2)}) async-start(), calls=%async_computation.5 | async-start | bytes 2359296 | tf_op jit(solution)/shard_map/all_gather | solution.py:13
  116.4 157.2 %reduce-scatter.2.cloned.1.call-start = ((), (), s32[]{:S(2)}) async-start(), calls=%async_computation.3 | async-start | bytes 4718592 | tf_op jit(solution)/shard_map/reduce_scatter | solution.py:111
  116.4 2.7 copy-start.1
  119.1 175.9 %all-reduce.2.cloned.1.call-start = ((), (), s32[]{:S(2)}) async-start(), calls=%async_computation.1 | async-start | bytes 1048576 | tf_op jit(solution)/shard_map/psum | solution.py:78
  119.2 10.2 %collective-permute-start = (bf16[256,512]{1,0:T(8,128)(2,1)S(1)}, bf16[256,512]{1,0:T(8,128)(2,1)S(1)}, u32[]{:S(2)}, u32[]{:S(2)}) collective-permute-start(bf16[256,512]{1,0:T(8,128)(2,1)S(1)} %copy-done.1), channel_id=1, source_target_pairs={{0,2},{2,4},{4,6},{6,8},{8,10},{10,12},{12,14},{14,0},{1,3},{3,5},... | collective-permute-start | bytes 786440 | tf_op jit(solution)/shard_map/ppermute | solution.py:71
  129.3 13.6 %collective-permute-start.1 = (bf16[256,512]{1,0:T(8,128)(2,1)S(1)}, bf16[256,512]{1,0:T(8,128)(2,1)S(1)}, u32[]{:S(2)}, u32[]{:S(2)}) collective-permute-start(bf16[256,512]{1,0:T(8,128)(2,1)S(1)} %collective-permute-done), channel_id=1, source_target_pairs={{0,2},{2,4},{4,6},{6,8},{8,10},{10,12},{12,14},{14,0},{1,3},{3,5},... | collective-permute-start | bytes 786440 | tf_op jit(solution)/shard_map/ppermute | solution.py:71
  142.9 13.8 %collective-permute-start.2 = (bf16[256,512]{1,0:T(8,128)(2,1)S(1)}, bf16[256,512]{1,0:T(8,128)(2,1)S(1)}, u32[]{:S(2)}, u32[]{:S(2)}) collective-permute-start(bf16[256,512]{1,0:T(8,128)(2,1)S(1)} %collective-permute-done.1), channel_id=1, source_target_pairs={{0,2},{2,4},{4,6},{6,8},{8,10},{10,12},{12,14},{14,0},{1,3},{3,5},... | collective-permute-start | bytes 786440 | tf_op jit(solution)/shard_map/ppermute | solution.py:71
  156.7 13.6 %collective-permute-start.3 = (bf16[256,512]{1,0:T(8,128)(2,1)S(1)}, bf16[256,512]{1,0:T(8,128)(2,1)S(1)}, u32[]{:S(2)}, u32[]{:S(2)}) collective-permute-start(bf16[256,512]{1,0:T(8,128)(2,1)S(1)} %collective-permute-done.2), channel_id=1, source_target_pairs={{0,2},{2,4},{4,6},{6,8},{8,10},{10,12},{12,14},{14,0},{1,3},{3,5},... | collective-permute-start | bytes 786440 | tf_op jit(solution)/shard_map/ppermute | solution.py:71
  170.3 10.5 %collective-permute-start.4 = (bf16[256,512]{1,0:T(8,128)(2,1)S(1)}, bf16[256,512]{1,0:T(8,128)(2,1)S(1)}, u32[]{:S(2)}, u32[]{:S(2)}) collective-permute-start(bf16[256,512]{1,0:T(8,128)(2,1)S(1)} %collective-permute-done.3), channel_id=1, source_target_pairs={{0,2},{2,4},{4,6},{6,8},{8,10},{10,12},{12,14},{14,0},{1,3},{3,5},... | collective-permute-start | bytes 786440 | tf_op jit(solution)/shard_map/ppermute | solution.py:71
  180.8 9.3 %collective-permute-start.5 = (bf16[256,512]{1,0:T(8,128)(2,1)S(1)}, bf16[256,512]{1,0:T(8,128)(2,1)}, u32[]{:S(2)}, u32[]{:S(2)}) collective-permute-start(bf16[256,512]{1,0:T(8,128)(2,1)S(1)} %collective-permute-done.4), channel_id=1, source_target_pairs={{0,2},{2,4},{4,6},{6,8},{8,10},{10,12},{12,14},{14,0},{1,3},{3,5},... | collective-permute-start | bytes 786440 | tf_op jit(solution)/shard_map/ppermute | solution.py:71
  190.1 16.3 %collective-permute-start.6 = (bf16[256,512]{1,0:T(8,128)(2,1)}, bf16[256,512]{1,0:T(8,128)(2,1)}, u32[]{:S(2)}, u32[]{:S(2)}) collective-permute-start(bf16[256,512]{1,0:T(8,128)(2,1)} %collective-permute-done.5), channel_id=1, source_target_pairs={{0,2},{2,4},{4,6},{6,8},{8,10},{10,12},{12,14},{14,0},{1,3},{3,5},... | collective-permute-start | bytes 786440 | tf_op jit(solution)/shard_map/ppermute | solution.py:71
  190.1 22.5 %copy-start.4 = (bf16[128,512]{1,0:T(8,128)(2,1)S(1)}, bf16[128,512]{1,0:T(8,128)(2,1)}, u32[]{:S(2)}) copy-start(bf16[128,512]{1,0:T(8,128)(2,1)} %param.11) | copy-start | bytes 393220
  210.6 2.0 copy-start.3
  219.1 4.7 %copy-start.6 = (bf16[128,512]{1,0:T(8,128)(2,1)S(1)}, bf16[128,512]{1,0:T(8,128)(2,1)}, u32[]{:S(2)}) copy-start(bf16[128,512]{1,0:T(8,128)(2,1)} %param.10) | copy-start | bytes 393220
Sparse Core Ops, SparseCore 0:
  10.7 51.9 all-gather.7
  64.9 47.7 all-gather.5
  116.5 58.8 all-gather.9
  178.9 94.6 reduce-scatter.1
  276.5 18.4 all-reduce.1
